TPU v7x, 128 devices: a whole 4x4x4 slice. The times are simulated.
128 devices in a mesh: seq: 32 (over z, y, core), head: 4 (over x).
Axes of the slice: x: 4, y: 4, z: 4, core: 2. Of those that a mesh axis runs over, the one named last changes fastest.
Arguments:
- tokens: bfloat16 [16384, 4096], P('seq'), may hold values from -6 to 6
- w_query: bfloat16 [4096, 2048], P('seq', 'head'), may hold values from -0.09375 to 0.09375
- w_key: bfloat16 [4096, 2048], P('seq', 'head'), may hold values from -0.09375 to 0.09375
- w_value: bfloat16 [4096, 2048], P('seq', 'head'), may hold values from -0.09375 to 0.09375
- omega_seed: int32 [16, 128, 256], P('head'), may hold values from -4 to 4
- grad_out: bfloat16 [16384, 2048], P('seq', 'head'), may hold values from -6 to 6
Outputs:
- input_grad: bfloat16 [16384, 4096], P('seq', 'head')
- query_wgrad: float32 [4096, 2048], P('seq', 'head')
- key_wgrad: float32 [4096, 2048], P('seq', 'head')
- value_wgrad: float32 [4096, 2048], P('seq', 'head')
Inputs may be any that keep to these rules, and one draw needn't show every extreme that they name: `omega_seed`: the feature seeds are small whole numbers.
All inputs are finite; a program needn't handle non-finite values.
Results may differ from a plain program's by a relative error of at most 0.02.
Values may be sent and summed in bfloat16 or wider, within the bound.
No kernel may reach another device: no remote copies, remote signals or barrier semaphores. Data moves between devices by JAX's collectives and lax.ppermute only.
A program may use at most 128 MiB of HBM per device.

v0:
```python
import math
import jax
import jax.numpy as jnp
from jax import lax
from jax.sharding import PartitionSpec as P

exact_arithmetic_mode = lax.Precision.HIGHEST
seed_step = 0.4


def carried_in(shard, axis, join, neutral):
    place = lax.axis_index(axis)
    gathered = jax.tree.map(
        lambda a, kind: lax.all_gather(a.astype(kind), axis), shard, (jnp.bfloat16, jnp.bfloat16)
    )
    state = jax.tree.map(lambda a, e: jnp.zeros_like(a) + jnp.asarray(e, a.dtype), shard, neutral)

    def one(hop, state):
        return join(
            state,
            jax.tree.map(
                lambda a, own: lax.dynamic_index_in_dim(a, hop, 0, False).astype(own.dtype),
                gathered,
                shard,
            ),
        )

    return lax.fori_loop(0, place, one, state)


def carried_in_2(shard, axis, join, neutral):
    count = lax.axis_size(axis)
    place = lax.axis_index(axis)
    ahead = count - 1 - place
    gathered = jax.tree.map(
        lambda a, kind: lax.all_gather(a.astype(kind), axis),
        shard,
        jax.tree.map(lambda a: jnp.bfloat16 if a.dtype == jnp.float32 else a.dtype, shard),
    )
    state = jax.tree.map(lambda a, e: jnp.zeros_like(a) + jnp.asarray(e, a.dtype), shard, neutral)

    def one(hop, state):
        source = count - 1 - hop
        return join(
            state,
            jax.tree.map(
                lambda a, own: lax.dynamic_index_in_dim(a, source, 0, False).astype(own.dtype),
                gathered,
                shard,
            ),
        )

    return lax.fori_loop(0, ahead, one, state)


def feature_map(scaled, projection):
    projected = jnp.einsum("htd,hdm->htm", scaled, projection, precision=exact_arithmetic_mode)
    return jnp.exp(projected - 0.5 * jnp.sum(scaled * scaled, -1, keepdims=True)) / math.sqrt(
        projection.shape[-1]
    )


def feature_grad(upstream, features, scaled, projection):
    weighted = upstream * features
    projected = jnp.einsum("htm,hdm->htd", weighted, projection, precision=exact_arithmetic_mode)
    return (projected - jnp.sum(weighted, -1, keepdims=True) * scaled) * scaled.shape[-1] ** (-0.25)


def add_states(earlier, later_part):
    return (earlier[0] + later_part[0], earlier[1] + later_part[1])


def head_major(value_matrix, heads_here):
    tok_rows = value_matrix.shape[0]
    return value_matrix.astype(jnp.float32).reshape(tok_rows, heads_here, -1).transpose(1, 0, 2)


def token_major(value_matrix):
    return value_matrix.transpose(1, 0, 2).reshape(value_matrix.shape[1], -1).astype(jnp.bfloat16)


def back_product(grads, weight):
    return lax.dot_general(
        grads, weight, (((1,), (1,)), ((), ())), preferred_element_type=jnp.float32
    )


def projection_term(tokens, grads):
    return lax.dot_general(
        tokens, grads, (((0,), (0,)), ((), ())), preferred_element_type=jnp.float32
    )


def per_device(tokens, w_query, w_key, w_value, omega_seed, grad_out):
    heads_here = omega_seed.shape[0]
    head_size = omega_seed.shape[1]
    full_query, full_key, full_value = (
        lax.all_gather(w_query, "seq", axis=0, tiled=True),
        lax.all_gather(w_key, "seq", axis=0, tiled=True),
        lax.all_gather(w_value, "seq", axis=0, tiled=True),
    )
    query_act = jnp.dot(tokens, full_query, preferred_element_type=jnp.float32).astype(jnp.bfloat16)
    key_act = jnp.dot(tokens, full_key, preferred_element_type=jnp.float32).astype(jnp.bfloat16)
    value_act = jnp.dot(tokens, full_value, preferred_element_type=jnp.float32).astype(jnp.bfloat16)
    projection = omega_seed.astype(jnp.float32) * seed_step
    scale_in = head_size ** (-0.25)
    query_scaled = head_major(query_act, heads_here) * scale_in
    key_scaled = head_major(key_act, heads_here) * scale_in
    value_matrix = head_major(value_act, heads_here)
    upstream = head_major(grad_out, heads_here)
    query_feature_rows = feature_map(query_scaled, projection)
    source_embedding_entries = feature_map(key_scaled, projection)
    tok_rows = tokens.shape[0]
    causal = jnp.tril(jnp.ones((tok_rows, tok_rows), jnp.float32))
    block_local_states = jnp.einsum(
        "vzn,vza->vna", source_embedding_entries, value_matrix, precision=exact_arithmetic_mode
    )
    local_totals = jnp.sum(source_embedding_entries, 1)
    zero_states = jnp.zeros_like(block_local_states)
    zero_totals = jnp.zeros_like(local_totals)
    prefix_carried_outer, prefix_normaliser_accrual = carried_in(
        (block_local_states, local_totals), "seq", add_states, (zero_states, zero_totals)
    )
    attention_scores = (
        jnp.einsum(
            "htm,hsm->hts",
            query_feature_rows,
            source_embedding_entries,
            precision=exact_arithmetic_mode,
        )
        * causal
    )
    attention_numerator = jnp.einsum(
        "xyw,xwc->xyc", attention_scores, value_matrix, precision=exact_arithmetic_mode
    ) + jnp.einsum(
        "sji,six->sjx", query_feature_rows, prefix_carried_outer, precision=exact_arithmetic_mode
    )
    normer = jnp.sum(attention_scores, -1) + jnp.einsum(
        "htm,hm->ht", query_feature_rows, prefix_normaliser_accrual, precision=exact_arithmetic_mode
    )
    output = attention_numerator / normer[..., None]
    dividend_cotangent = upstream / normer[..., None]
    normaliser_cotangent = -jnp.sum(upstream * output, -1) / normer
    couplewise_products = (
        jnp.einsum(
            "htd,hsd->hts", dividend_cotangent, value_matrix, precision=exact_arithmetic_mode
        )
        + normaliser_cotangent[..., None]
    ) * causal
    target_embedding_cotangent = (
        jnp.einsum(
            "mez,mzo->meo",
            couplewise_products,
            source_embedding_entries,
            precision=exact_arithmetic_mode,
        )
        + jnp.einsum(
            "zrc,zfc->zrf",
            dividend_cotangent,
            prefix_carried_outer,
            precision=exact_arithmetic_mode,
        )
        + normaliser_cotangent[..., None] * prefix_normaliser_accrual[:, None, :]
    )
    query16 = token_major(
        feature_grad(target_embedding_cotangent, query_feature_rows, query_scaled, projection)
    )
    subsequent_local_states = jnp.einsum(
        "opu,opc->ouc", query_feature_rows, dividend_cotangent, precision=exact_arithmetic_mode
    )
    later_totals = jnp.einsum(
        "htm,ht->hm", query_feature_rows, normaliser_cotangent, precision=exact_arithmetic_mode
    )
    subsequent_states, subsequent_sum = carried_in_2(
        (subsequent_local_states, later_totals), "seq", add_states, (zero_states, zero_totals)
    )
    key_feature_gradient = (
        jnp.einsum(
            "ykl,yku->ylu", couplewise_products, query_feature_rows, precision=exact_arithmetic_mode
        )
        + jnp.einsum(
            "bgq,bxq->bgx", value_matrix, subsequent_states, precision=exact_arithmetic_mode
        )
        + subsequent_sum[:, None, :]
    )
    value_gradient_rows = jnp.einsum(
        "vkm,vky->vmy", attention_scores, dividend_cotangent, precision=exact_arithmetic_mode
    ) + jnp.einsum(
        "tjr,tro->tjo", source_embedding_entries, subsequent_states, precision=exact_arithmetic_mode
    )
    key16 = token_major(
        feature_grad(key_feature_gradient, source_embedding_entries, key_scaled, projection)
    )
    value16 = token_major(value_gradient_rows)
    joined = jnp.concatenate([query16, key16, value16], 1)
    weight_total = lax.psum_scatter(
        projection_term(tokens, joined).astype(jnp.bfloat16), "seq", scatter_dimension=0, tiled=True
    ).astype(jnp.float32)
    columns = query16.shape[1]
    query_wgrad = weight_total[:, :columns]
    key_wgrad = weight_total[:, columns : 2 * columns]
    value_wgrad = weight_total[:, 2 * columns :]
    partial_input = (
        back_product(query16, full_query)
        + back_product(key16, full_key)
        + back_product(value16, full_value)
    )
    input_grad = lax.psum_scatter(
        partial_input.astype(jnp.bfloat16), "head", scatter_dimension=1, tiled=True
    )
    return (input_grad, query_wgrad, key_wgrad, value_wgrad)


def solution(mesh):
    placed = (
        P("seq", None),
        P("seq", "head"),
        P("seq", "head"),
        P("seq", "head"),
        P("head", None, None),
        P("seq", "head"),
    )
    return jax.shard_map(
        per_device,
        mesh=mesh,
        in_specs=placed,
        out_specs=(P("seq", "head"), P("seq", "head"), P("seq", "head"), P("seq", "head")),
        check_vma=False,
    )
```

profile of v0, /device:TPU:1, one launch (start us, length us, event | category | flops | bytes accessed | tf_op | source)
XLA Modules:
  0.0 566.0 jit_solution(16715974828505819920)
XLA Ops:
  9.4 50.6 %all-gather.16.cloned.1.call-done = bf16[4096,512]{1,0:T(8,128)(2,1)} async-done(((bf16[128,512]{1,0:T(8,128)(2,1)}), bf16[4096,512]{1,0:T(8,128)(2,1)}) %all-gather.16.cloned.1.call-update) | async-done | bytes 4194320 | tf_op jit(solution)/shard_map/all_gather | solution.py:100
  60.1 5.8 %convolution_convert_fusion.1 = bf16[512,512]{0,1:T(8,128)(2,1)S(1)} fusion(bf16[512,4096]{1,0:T(8,128)(2,1)} %param.10, bf16[4096,512]{1,0:T(8,128)(2,1)} %all-gather.16.cloned.1.call-done), kind=kOutput, calls=%fused_computation.45 | convolution fusion | flops 2147745792 | bytes 8912896 | tf_op jit(solution)/shard_map/dot_general | solution.py:104
  67.0 40.8 %all-gather.14.cloned.1.call-done = bf16[4096,512]{1,0:T(8,128)(2,1)} async-done(((bf16[128,512]{1,0:T(8,128)(2,1)}), bf16[4096,512]{1,0:T(8,128)(2,1)}) %all-gather.14.cloned.1.call-update) | async-done | bytes 4194320 | tf_op jit(solution)/shard_map/all_gather | solution.py:99
  107.8 5.8 %convolution_convert_fusion.2 = bf16[512,512]{0,1:T(8,128)(2,1)S(1)} fusion(bf16[512,4096]{1,0:T(8,128)(2,1)} %param.10, bf16[4096,512]{1,0:T(8,128)(2,1)} %all-gather.14.cloned.1.call-done), kind=kOutput, calls=%fused_computation.46 | convolution fusion | flops 2147745792 | bytes 8912896 | tf_op jit(solution)/shard_map/dot_general | solution.py:103
  113.8 2.3 fusion.74
  120.6 24.0 %all-gather.4 = bf16[32,4,256]{2,1,0:T(4,128)(2,1)S(1)} all-gather(bf16[1,4,256]{2,1,0:T(4,128)(2,1)S(1)} %bitcast.157), channel_id=3, replica_groups=mesh['seq'=32,'head'=4] {'seq'}, dimensions={0}, use_global_device_ids=true | all-gather | bytes 67584 | tf_op jit(solution)/shard_map/all_gather | solution.py:14
  144.6 11.0 %all-gather.12.cloned.1.call-done = bf16[4096,512]{1,0:T(8,128)(2,1)} async-done(((bf16[128,512]{1,0:T(8,128)(2,1)}), bf16[4096,512]{1,0:T(8,128)(2,1)}) %all-gather.12.cloned.1.call-update) | async-done | bytes 4194320 | tf_op jit(solution)/shard_map/all_gather | solution.py:98
  155.6 5.9 %convolution_convert_fusion.3 = bf16[512,512]{0,1:T(8,128)(2,1)S(1)} fusion(bf16[512,4096]{1,0:T(8,128)(2,1)} %param.10, bf16[4096,512]{1,0:T(8,128)(2,1)} %all-gather.12.cloned.1.call-done), kind=kOutput, calls=%fused_computation.47 | convolution fusion | flops 2147745792 | bytes 8912896 | tf_op jit(solution)/shard_map/dot_general | solution.py:102
  161.7 2.0 exponential_multiply_fusion.1
  163.7 5.2 multiply_reduce_fusion
  169.0 41.5 %all-gather.18.cloned.1.call-done = bf16[128,256,128]{2,1,0:T(8,128)(2,1)} async-done(((bf16[4,256,128]{2,1,0:T(8,128)(2,1)}), bf16[128,256,128]{2,1,0:T(8,128)(2,1)}) %all-gather.18.cloned.1.call-update) | async-done | bytes 8388624 | tf_op jit(solution)/shard_map/all_gather | solution.py:14
  211.3 2.0 while.26
  211.3 2.0 convert_add_fusion.8
  214.5 3.9 convolution_convert_fusion.4
  218.5 2.6 fusion.77
  221.1 4.2 fusion.39
  227.2 90.3 %all-gather.5 = bf16[32,4,256]{2,1,0:T(4,128)(2,1)S(1)} all-gather(bf16[1,4,256]{2,1,0:T(4,128)(2,1)S(1)} %bitcast.156), channel_id=5, replica_groups=mesh['seq'=32,'head'=4] {'seq'}, dimensions={0}, use_global_device_ids=true | all-gather | bytes 67584 | tf_op jit(solution)/shard_map/all_gather | solution.py:36
  317.5 1.9 fusion.52
  319.4 4.3 fusion.2
  323.7 2.4 fusion.75
  326.1 2.2 fusion.29
  328.3 5.6 fusion.1
  334.0 33.3 %while.27 = (s32[]{:T(128)}, f32[4,256,128]{2,1,0:T(8,128)S(1)}, f32[4,256]{1,0:T(4,128)S(1)}, s32[]{:T(128)}, bf16[32,4,256,128]{3,2,1,0:T(8,128)(2,1)}, /*inde...) while((s32[]{:T(128)}, f32[4,256,128]{2,1,0:T(8,128)S(1)}, ...), condition=%wide.region_9.10_spmd, body=%wide.region_8.9_spmd.sunk | while | flops 264198 | bytes 1321123 | solution.py:53
  367.3 3.0 fusion.80
  370.4 7.0 %fusion.30 = bf16[4,512,128]{1,2,0:T(8,128)(2,1)S(1)} fusion(f32[4,512,128]{1,2,0:T(8,128)S(1)} %fusion.80, f32[4,512,512]{1,2,0:T(8,128)} %get-tuple-element.159, f32[512,512]{0,1:T(8,128)S(1)} %fusion.50, f32[4,512]{1,0:T(4,128)S(1)} %bitcast_add_fusion, f32[512,512]{0,1:T(8,128)S(1)} %copy-done.6), kind=kOutput, calls=%fused_computation.44 | convolution fusion | flops 1612447744 | bytes 7872512 | tf_op jit(solution)/shard_map/vkm,vky->vmy/dot_general | solution.py:186
  380.3 11.5 %fusion = bf16[4096,1536]{0,1:T(8,128)(2,1)} fusion(bf16[512,4096]{1,0:T(8,128)(2,1)S(1)} %copy-done.26, bf16[512,512]{0,1:T(8,128)(2,1)S(1)} %bitcast.146, bf16[512,512]{0,1:T(8,128)(2,1)S(1)} %bitcast.148, bf16[512,512]{0,1:T(8,128)(2,1)S(1)} %bitcast.144), kind=kOutput, calls=%fused_computation.5 | convolution fusion | flops 6453460992 | bytes 18350080 | tf_op jit(solution)/shard_map/dot_general | solution.py:89
  391.7 16.6 %copy.89 = bf16[4096,1536]{1,0:T(8,128)(2,1)} copy(bf16[4096,1536]{0,1:T(8,128)(2,1)} %fusion) | data formatting | bytes 25165824
  408.7 4.7 fusion.78
  413.5 5.9 %fusion.79 = f32[512,4096]{1,0:T(8,128)} fusion(bf16[512,512]{0,1:T(8,128)(2,1)S(1)} %bitcast.149, bf16[4096,512]{1,0:T(8,128)(2,1)S(1)} %copy-done.20), kind=kOutput, calls=%fused_computation.99 | convolution fusion | flops 2147483648 | bytes 13107200 | tf_op jit(solution)/shard_map/dot_general | solution.py:83
  419.4 8.3 %add_convert_fusion = bf16[512,4096]{1,0:T(8,128)(2,1)} fusion(f32[512,4096]{1,0:T(8,128)S(1)} %fusion.78, f32[512,4096]{1,0:T(8,128)} %fusion.79, bf16[512,512]{0,1:T(8,128)(2,1)S(1)} %bitcast.147, bf16[4096,512]{1,0:T(8,128)(2,1)S(1)} %copy-done.19), kind=kOutput, calls=%fused_computation.6 | convolution fusion | flops 2153775104 | bytes 25690112 | tf_op jit(solution)/shard_map/dot_general | solution.py:83
  427.8 80.2 %reduce-scatter.7.cloned.1.call-done = bf16[128,1536]{1,0:T(8,128)(2,1)} async-done(((bf16[4096,1536]{1,0:T(8,128)(2,1)}), bf16[128,1536]{1,0:T(8,128)(2,1)}) %reduce-scatter.7.cloned.1.call-update) | async-done | bytes 393232
  511.7 46.9 %reduce-scatter.5.cloned.1.call-done = bf16[512,1024]{1,0:T(8,128)(2,1)} async-done(((bf16[512,4096]{1,0:T(8,128)(2,1)}), bf16[512,1024]{1,0:T(8,128)(2,1)}) %reduce-scatter.5.cloned.1.call-update) | async-done | bytes 1048592 | tf_op jit(solution)/shard_map/reduce_scatter | solution.py:208
  (156 shorter events, 51.6 us)
Async XLA Ops:
  7.2 52.9 %all-gather.16.cloned.1.call-start = ((), (), s32[]{:S(2)}) async-start(), calls=%async_computation.4 | async-start | bytes 4325376 | tf_op jit(solution)/shard_map/all_gather | solution.py:100
  7.9 99.9 %all-gather.14.cloned.1.call-start = ((), (), s32[]{:S(2)}) async-start(), calls=%async_computation.3 | async-start | bytes 4325376 | tf_op jit(solution)/shard_map/all_gather | solution.py:99
  8.6 146.9 %all-gather.12.cloned.1.call-start = ((), (), s32[]{:S(2)}) async-start(), calls=%async_computation.2 | async-start | bytes 4325376 | tf_op jit(solution)/shard_map/all_gather | solution.py:98
  9.4 201.1 %all-gather.18.cloned.1.call-start = ((), (), s32[]{:S(2)}) async-start(), calls=%async_computation.6 | async-start | bytes 8650752 | tf_op jit(solution)/shard_map/all_gather | solution.py:14
  67.0 49.1 %copy-start.12 = (bf16[512,4,128]{2,0,1:T(8,128)(2,1)}, bf16[512,4,128]{2,0,1:T(8,128)(2,1)S(1)}, u32[]{:S(2)}) copy-start(bf16[512,4,128]{2,0,1:T(8,128)(2,1)S(1)} %copy.43) | copy-start | bytes 1572868
  67.0 46.8 %copy-start.7 = (s32[4,128,256]{2,1,0:T(8,128)S(1)}, s32[4,128,256]{2,1,0:T(8,128)}, u32[]{:S(2)}) copy-start(s32[4,128,256]{2,1,0:T(8,128)} %param.14) | copy-start | bytes 1572868
  113.6 2.5 copy-start.15
  113.7 5.7 %copy-start.25 = (bf16[512,512]{1,0:T(8,128)(2,1)S(1)}, bf16[512,512]{1,0:T(8,128)(2,1)}, u32[]{:S(2)}) copy-start(bf16[512,512]{1,0:T(8,128)(2,1)} %param.15) | copy-start | bytes 1572868
  119.3 214.7 %all-gather.20.cloned.1.call-start = ((), (), s32[]{:S(2)}) async-start(), calls=%async_computation.7 | async-start | bytes 8650752 | tf_op jit(solution)/shard_map/all_gather | solution.py:36
  155.6 6.1 %copy-start.8 = (s32[4,128,256]{2,1,0:T(8,128)S(1)}, s32[4,128,256]{2,1,0:T(8,128)}, u32[]{:S(2)}) copy-start(s32[4,128,256]{2,1,0:T(8,128)} %param.14) | copy-start | bytes 1572868
  161.5 2.2 copy-start.17
  161.5 2.2 copy-start.1
  218.4 289.5 %reduce-scatter.7.cloned.1.call-start = ((), (), s32[]{:S(2)}) async-start(), calls=%async_computation.8 | async-start | bytes 12976128
  218.5 2.6 copy-start.5
  221.1 96.4 %copy-start.13 = (bf16[512,4,128]{2,0,1:T(8,128)(2,1)S(1)}, bf16[512,4,128]{2,0,1:T(8,128)(2,1)}, u32[]{:S(2)}) copy-start(bf16[512,4,128]{2,0,1:T(8,128)(2,1)} %copy-done.12) | copy-start | bytes 1572868
  225.3 94.1 %copy-start.2 = (f32[4,512,256]{1,2,0:T(8,128)S(1)}, f32[4,512,256]{1,2,0:T(8,128)}, u32[]{:S(2)}) copy-start(f32[4,512,256]{1,2,0:T(8,128)} %copy-done) | copy-start | bytes 6291460
  319.4 4.3 copy-start.4
  323.7 2.4 copy-start.9
  323.7 2.4 copy-start.18
  334.0 36.4 %copy-start.6 = (f32[512,512]{0,1:T(8,128)S(1)}, f32[512,512]{0,1:T(8,128)}, u32[]{:S(2)}) copy-start(f32[512,512]{0,1:T(8,128)} %copy.36) | copy-start | bytes 3145732
  370.4 7.0 %copy-start.3 = (f32[4,512,256]{1,2,0:T(8,128)S(1)}, f32[4,512,256]{1,2,0:T(8,128)}, u32[]{:S(2)}) copy-start(f32[4,512,256]{1,2,0:T(8,128)} %copy-done) | copy-start | bytes 6291460
  370.4 7.0 %copy-start.11 = (f32[4,512,256]{1,2,0:T(8,128)S(1)}, f32[4,512,256]{1,2,0:T(8,128)}, u32[]{:S(2)}) copy-start(f32[4,512,256]{1,2,0:T(8,128)} %fusion.1) | copy-start | bytes 6291460
  370.4 7.0 %copy-start.14 = (bf16[512,4,128]{2,0,1:T(8,128)(2,1)S(1)}, bf16[512,4,128]{2,0,1:T(8,128)(2,1)}, u32[]{:S(2)}) copy-start(bf16[512,4,128]{2,0,1:T(8,128)(2,1)} %copy-done.12) | copy-start | bytes 1572868
  377.4 1.5 copy-start.10
  377.4 1.5 copy-start.16
  377.4 2.8 copy-start.21
  377.4 2.8 copy-start.26
  380.2 11.5 %copy-start.22 = (bf16[512,4,128]{0,2,1:T(8,128)(2,1)}, bf16[512,4,128]{0,2,1:T(8,128)(2,1)S(1)}, u32[]{:S(2)}) copy-start(bf16[512,4,128]{0,2,1:T(8,128)(2,1)S(1)} %fusion.28) | copy-start | bytes 1572868
  408.4 5.1 copy-start.23
  408.4 150.3 %reduce-scatter.5.cloned.1.call-start = ((), (), s32[]{:S(2)}) async-start(), calls=%async_computation.5 | async-start | bytes 5242880 | tf_op jit(solution)/shard_map/reduce_scatter | solution.py:208
  408.7 4.8 copy-start.20
  413.5 5.9 %copy-start.19 = (bf16[4096,512]{1,0:T(8,128)(2,1)S(1)}, bf16[4096,512]{1,0:T(8,128)(2,1)}, u32[]{:S(2)}) copy-start(bf16[4096,512]{1,0:T(8,128)(2,1)} %all-gather.16.cloned.1.call-done) | copy-start | bytes 12582916
  (2 other events, 2.1 us)
Sparse Core Ops, SparseCore 0:
  10.2 49.7 all-gather.15
  62.3 45.4 all-gather.13
  110.1 45.4 all-gather.11
  158.3 52.1 all-gather.17
  218.6 110.8 all-gather.19
  408.5 99.3 reduce-scatter.6
  510.9 47.7 reduce-scatter.4
where the time goes:
time: 574 us; the launch traced here: 566 us
  waiting for transfers between devices  273 us (48%)
  blocking collectives  114 us (20%)
  matrix products  102 us (18%)
  other arithmetic  35 us (6%)
  local copies, waits for them, and re-layouts  25 us (4%)
  between operations  15.2 us (3%)
    all_gather x1, blocking collectives, carried_in_2(): lax.all_gather(a.astype(kind), axis)  90.3 us
    unnamed x8, waiting for transfers between devices  82.3 us
    all_gather x1, waiting for transfers between devices, per_device(): lax.all_gather(w_value, 'seq', axis=0, tiled=True)  50.6 us
    reduce_scatter x1, waiting for transfers between devices, per_device(): lax.psum_scatter(partial_input.astype(jnp.bfloat16), 'head', scatter_dime...  46.9 us
    all_gather x1, waiting for transfers between devices, carried_in(): lax.all_gather(a.astype(kind), axis)  41.5 us
    all_gather x1, waiting for transfers between devices, per_device(): lax.all_gather(w_key, 'seq', axis=0, tiled=True)  40.8 us
    add x62, other arithmetic, add_states(): return (earlier[0] + later_part[0], earlier[1] + later_part[1])  34.6 us
    all_gather x1, blocking collectives, carried_in(): lax.all_gather(a.astype(kind), axis)  24 us
  transfers between devices with their start and end apart: 7, of which 6 were waited for; matrix products, arithmetic and copies ran while one was open for 14% of the time, Pallas kernels for 0%

commit v1 on v0

--- a/solution.py
+++ b/solution.py
@@ -97,7 +97,9 @@
     full_query, full_key, full_value = (
         lax.all_gather(w_query, "seq", axis=0, tiled=True),
         lax.all_gather(w_key, "seq", axis=0, tiled=True),
-        lax.all_gather(w_value, "seq", axis=0, tiled=True),
+        jnp.concatenate(
+            lax.all_to_all(jnp.stack([w_value] * lax.axis_size("seq")), "seq", 0, 0), axis=0
+        ),
     )
     query_act = jnp.dot(tokens, full_query, preferred_element_type=jnp.float32).astype(jnp.bfloat16)
     key_act = jnp.dot(tokens, full_key, preferred_element_type=jnp.float32).astype(jnp.bfloat16)

time: 574 us -> 549 us (0.956)
  waiting for transfers between devices: 273 us -> 183 us
  blocking collectives: 114 us -> 181 us
    all_to_all x0 -> x1, blocking collectives: none -> 67.7 us  [per_device(): lax.all_to_all(jnp.stack([w_value] * lax.axis_size('seq')), 'seq', 0, 0)]
    all_gather x1 -> x0, waiting for transfers between devices: 50.6 us -> none  [per_device(): lax.all_gather(w_value, 'seq', axis=0, tiled=True)]
    all_gather x1, waiting for transfers between devices: 40.8 us -> 0.98 us  [per_device(): lax.all_gather(w_key, 'seq', axis=0, tiled=True)]
    unnamed x8 -> x7, waiting for transfers between devices: 82.3 us -> 81.6 us
    unnamed x59 -> x63, local copies, waits for them, and re-layouts: 22.6 us -> 22.6 us
  transfers between devices with their start and end apart: 7 -> 6, of which waited for: 6 -> 5; matrix products, arithmetic and copies ran while one was open for 14% -> 14% of each run, Pallas kernels for 0% -> 0%
where the time goes in v1:
time: 549 us; the launch traced here: 540 us
  waiting for transfers between devices  183 us (33%)
  blocking collectives  181 us (33%)
  matrix products  98.7 us (18%)
  other arithmetic  35 us (6%)
  local copies, waits for them, and re-layouts  26.4 us (5%)
  between operations  15.2 us (3%)
    all_gather x1, blocking collectives, carried_in_2(): lax.all_gather(a.astype(kind), axis)  89.9 us
    unnamed x7, waiting for transfers between devices  81.6 us
    all_to_all x1, blocking collectives, per_device(): lax.all_to_all(jnp.stack([w_value] * lax.axis_size('seq')), 'seq', 0, 0)  67.7 us
    reduce_scatter x1, waiting for transfers between devices, per_device(): lax.psum_scatter(partial_input.astype(jnp.bfloat16), 'head', scatter_dime...  46.8 us
    all_gather x1, waiting for transfers between devices, carried_in(): lax.all_gather(a.astype(kind), axis)  41.6 us
    add x62, other arithmetic, add_states(): return (earlier[0] + later_part[0], earlier[1] + later_part[1])  34.5 us
    all_gather x1, blocking collectives, carried_in(): lax.all_gather(a.astype(kind), axis)  23 us
    unnamed x63, local copies, waits for them, and re-layouts  22.6 us
  transfers between devices with their start and end apart: 6, of which 5 were waited for; matrix products, arithmetic and copies ran while one was open for 14% of the time, Pallas kernels for 0%

profile of v1, /device:TPU:1, one launch (start us, length us, event | category | flops | bytes accessed | tf_op | source)
XLA Modules:
  0.0 539.8 jit_solution(301825980744603139)
XLA Ops:
  10.1 67.7 %all_to_all.5 = bf16[32,128,512]{2,1,0:T(8,128)(2,1)S(1)} all-to-all(bf16[32,128,512]{2,1,0:T(8,128)(2,1)S(1)} %stack.2), channel_id=1, replica_groups=mesh['seq'=32,'head'=4] {'seq'}, dimensions={0} | all-to-all | bytes 8388608 | tf_op jit(solution)/shard_map/all_to_all | solution.py:101
  77.8 2.4 convolution_convert_fusion.1
  82.3 5.8 %convolution_convert_fusion.2 = bf16[512,512]{0,1:T(8,128)(2,1)S(1)} fusion(bf16[512,4096]{1,0:T(8,128)(2,1)} %param.10, bf16[4096,512]{1,0:T(8,128)(2,1)} %all-gather.13.cloned.1.call-done), kind=kOutput, calls=%fused_computation.46 | convolution fusion | flops 2147745792 | bytes 8912896 | tf_op jit(solution)/shard_map/dot_general | solution.py:105
  88.3 2.3 fusion.74
  95.1 23.0 %all-gather.4 = bf16[32,4,256]{2,1,0:T(4,128)(2,1)S(1)} all-gather(bf16[1,4,256]{2,1,0:T(4,128)(2,1)S(1)} %bitcast.160), channel_id=3, replica_groups=mesh['seq'=32,'head'=4] {'seq'}, dimensions={0}, use_global_device_ids=true | all-gather | bytes 67584 | tf_op jit(solution)/shard_map/all_gather | solution.py:14
  118.2 11.6 %all-gather.11.cloned.1.call-done = bf16[4096,512]{1,0:T(8,128)(2,1)} async-done(((bf16[128,512]{1,0:T(8,128)(2,1)}), bf16[4096,512]{1,0:T(8,128)(2,1)}) %all-gather.11.cloned.1.call-update) | async-done | bytes 4194320 | tf_op jit(solution)/shard_map/all_gather | solution.py:98
  129.8 5.9 %convolution_convert_fusion.3 = bf16[512,512]{0,1:T(8,128)(2,1)S(1)} fusion(bf16[512,4096]{1,0:T(8,128)(2,1)} %param.10, bf16[4096,512]{1,0:T(8,128)(2,1)} %all-gather.11.cloned.1.call-done), kind=kOutput, calls=%fused_computation.47 | convolution fusion | flops 2147745792 | bytes 8912896 | tf_op jit(solution)/shard_map/dot_general | solution.py:104
  135.9 2.0 exponential_multiply_fusion.1
  137.9 5.2 multiply_reduce_fusion
  143.2 41.6 %all-gather.15.cloned.1.call-done = bf16[128,256,128]{2,1,0:T(8,128)(2,1)} async-done(((bf16[4,256,128]{2,1,0:T(8,128)(2,1)}), bf16[128,256,128]{2,1,0:T(8,128)(2,1)}) %all-gather.15.cloned.1.call-update) | async-done | bytes 8388624 | tf_op jit(solution)/shard_map/all_gather | solution.py:14
  185.7 2.0 while.26
  185.7 2.0 convert_add_fusion.8
  188.8 3.9 convolution_convert_fusion.4
  192.8 2.6 fusion.77
  195.4 4.2 fusion.39
  199.7 1.9 fusion.61
  201.6 89.9 %all-gather.5 = bf16[32,4,256]{2,1,0:T(4,128)(2,1)S(1)} all-gather(bf16[1,4,256]{2,1,0:T(4,128)(2,1)S(1)} %bitcast.159), channel_id=5, replica_groups=mesh['seq'=32,'head'=4] {'seq'}, dimensions={0}, use_global_device_ids=true | all-gather | bytes 67584 | tf_op jit(solution)/shard_map/all_gather | solution.py:36
  291.4 1.9 fusion.52
  293.3 4.3 fusion.2
  297.7 2.4 fusion.75
  300.1 2.2 fusion.29
  302.2 5.6 %fusion.1 = f32[4,512,256]{1,2,0:T(8,128)} fusion(f32[4,512,256]{1,2,0:T(8,128)S(1)} %exponential_multiply_fusion.1, f32[4,512,512]{1,2,0:T(8,128)S(1)} %fusion.52, f32[4,512]{1,0:T(4,128)S(1)} %negate_divide_fusion, f32[512,512]{0,1:T(8,128)S(1)} %fusion.50), kind=kOutput, calls=%fused_computation.8 | convolution fusion | flops 3223322624 | bytes 9445376 | tf_op jit(solution)/shard_map/ykl,yku->ylu/dot_general | solution.py:180
  307.9 33.3 %while.27 = (s32[]{:T(128)}, f32[4,256,128]{2,1,0:T(8,128)S(1)}, f32[4,256]{1,0:T(4,128)S(1)}, s32[]{:T(128)}, bf16[32,4,256,128]{3,2,1,0:T(8,128)(2,1)}, /*inde...) while((s32[]{:T(128)}, f32[4,256,128]{2,1,0:T(8,128)S(1)}, ...), condition=%wide.region_9.10_spmd, body=%wide.region_8.9_spmd.sunk | while | flops 264198 | bytes 1321123 | solution.py:53
  341.3 3.0 fusion.80
  344.3 7.0 %fusion.30 = bf16[4,512,128]{1,2,0:T(8,128)(2,1)S(1)} fusion(f32[4,512,128]{1,2,0:T(8,128)S(1)} %fusion.80, f32[4,512,512]{1,2,0:T(8,128)} %get-tuple-element.159, f32[512,512]{0,1:T(8,128)S(1)} %fusion.50, f32[4,512]{1,0:T(4,128)S(1)} %bitcast_add_fusion, f32[512,512]{0,1:T(8,128)S(1)} %copy-done.6), kind=kOutput, calls=%fused_computation.44 | convolution fusion | flops 1612447744 | bytes 7872512 | tf_op jit(solution)/shard_map/vkm,vky->vmy/dot_general | solution.py:188
  354.2 11.5 %fusion = bf16[4096,1536]{0,1:T(8,128)(2,1)} fusion(bf16[512,4096]{1,0:T(8,128)(2,1)S(1)} %copy-done.28, bf16[512,512]{0,1:T(8,128)(2,1)S(1)} %bitcast.149, bf16[512,512]{0,1:T(8,128)(2,1)S(1)} %bitcast.151, bf16[512,512]{0,1:T(8,128)(2,1)S(1)} %bitcast.147), kind=kOutput, calls=%fused_computation.5 | convolution fusion | flops 6453460992 | bytes 18350080 | tf_op jit(solution)/shard_map/dot_general | solution.py:89
  365.7 16.7 %copy.89 = bf16[4096,1536]{1,0:T(8,128)(2,1)} copy(bf16[4096,1536]{0,1:T(8,128)(2,1)} %fusion) | data formatting | bytes 25165824
  382.7 4.7 fusion.78
  387.5 5.9 %fusion.79 = f32[512,4096]{1,0:T(8,128)} fusion(bf16[512,512]{0,1:T(8,128)(2,1)S(1)} %bitcast.152, bf16[4096,512]{1,0:T(8,128)(2,1)S(1)} %copy-done.21), kind=kOutput, calls=%fused_computation.99 | convolution fusion | flops 2147483648 | bytes 13107200 | tf_op jit(solution)/shard_map/dot_general | solution.py:83
  393.4 8.3 %add_convert_fusion = bf16[512,4096]{1,0:T(8,128)(2,1)} fusion(f32[512,4096]{1,0:T(8,128)S(1)} %fusion.78, f32[512,4096]{1,0:T(8,128)} %fusion.79, bf16[512,512]{0,1:T(8,128)(2,1)S(1)} %bitcast.150, bf16[4096,512]{1,0:T(8,128)(2,1)S(1)} %bitcast.140), kind=kOutput, calls=%fused_computation.6 | convolution fusion | flops 2153775104 | bytes 25690112 | tf_op jit(solution)/shard_map/dot_general | solution.py:83
  401.8 80.2 %reduce-scatter.7.cloned.1.call-done = bf16[128,1536]{1,0:T(8,128)(2,1)} async-done(((bf16[4096,1536]{1,0:T(8,128)(2,1)}), bf16[128,1536]{1,0:T(8,128)(2,1)}) %reduce-scatter.7.cloned.1.call-update) | async-done | bytes 393232
  485.7 46.8 %reduce-scatter.5.cloned.1.call-done = bf16[512,1024]{1,0:T(8,128)(2,1)} async-done(((bf16[512,4096]{1,0:T(8,128)(2,1)}), bf16[512,1024]{1,0:T(8,128)(2,1)}) %reduce-scatter.5.cloned.1.call-update) | async-done | bytes 1048592 | tf_op jit(solution)/shard_map/reduce_scatter | solution.py:210
  (159 shorter events, 51.4 us)
Async XLA Ops:
  7.2 75.1 %all-gather.13.cloned.1.call-start = ((), (), s32[]{:S(2)}) async-start(), calls=%async_computation.4 | async-start | bytes 4325376 | tf_op jit(solution)/shard_map/all_gather | solution.py:99
  7.9 121.9 %all-gather.11.cloned.1.call-start = ((), (), s32[]{:S(2)}) async-start(), calls=%async_computation.3 | async-start | bytes 4325376 | tf_op jit(solution)/shard_map/all_gather | solution.py:98
  8.7 176.2 %all-gather.15.cloned.1.call-start = ((), (), s32[]{:S(2)}) async-start(), calls=%async_computation.6 | async-start | bytes 8650752 | tf_op jit(solution)/shard_map/all_gather | solution.py:14
  10.1 67.8 %copy-start.27 = (bf16[512,4096]{1,0:T(8,128)(2,1)S(1)}, bf16[512,4096]{1,0:T(8,128)(2,1)}, u32[]{:S(2)}) copy-start(bf16[512,4096]{1,0:T(8,128)(2,1)} %param.10) | copy-start | bytes 12582916
  77.8 2.4 copy-start.7
  81.3 9.3 %copy-start.14 = (bf16[512,4,128]{2,0,1:T(8,128)(2,1)}, bf16[512,4,128]{2,0,1:T(8,128)(2,1)S(1)}, u32[]{:S(2)}) copy-start(bf16[512,4,128]{2,0,1:T(8,128)(2,1)S(1)} %copy.43) | copy-start | bytes 1572868
  81.3 7.0 %copy-start.9 = (s32[4,128,256]{2,1,0:T(8,128)S(1)}, s32[4,128,256]{2,1,0:T(8,128)}, u32[]{:S(2)}) copy-start(s32[4,128,256]{2,1,0:T(8,128)} %param.14) | copy-start | bytes 1572868
  88.1 2.5 copy-start.17
  88.1 5.7 %copy-start.26 = (bf16[512,512]{1,0:T(8,128)(2,1)S(1)}, bf16[512,512]{1,0:T(8,128)(2,1)}, u32[]{:S(2)}) copy-start(bf16[512,512]{1,0:T(8,128)(2,1)} %param.15) | copy-start | bytes 1572868
  93.8 214.1 %all-gather.17.cloned.1.call-start = ((), (), s32[]{:S(2)}) async-start(), calls=%async_computation.7 | async-start | bytes 8650752 | tf_op jit(solution)/shard_map/all_gather | solution.py:36
  129.8 6.1 %copy-start.10 = (s32[4,128,256]{2,1,0:T(8,128)S(1)}, s32[4,128,256]{2,1,0:T(8,128)}, u32[]{:S(2)}) copy-start(s32[4,128,256]{2,1,0:T(8,128)} %param.14) | copy-start | bytes 1572868
  135.7 2.2 copy-start.19
  135.7 2.2 copy-start.1
  192.8 289.2 %reduce-scatter.7.cloned.1.call-start = ((), (), s32[]{:S(2)}) async-start(), calls=%async_computation.8 | async-start | bytes 12976128
  192.8 2.6 copy-start.5
  195.4 96.0 %copy-start.15 = (bf16[512,4,128]{2,0,1:T(8,128)(2,1)S(1)}, bf16[512,4,128]{2,0,1:T(8,128)(2,1)}, u32[]{:S(2)}) copy-start(bf16[512,4,128]{2,0,1:T(8,128)(2,1)} %copy-done.14) | copy-start | bytes 1572868
  199.7 93.7 %copy-start.2 = (f32[4,512,256]{1,2,0:T(8,128)S(1)}, f32[4,512,256]{1,2,0:T(8,128)}, u32[]{:S(2)}) copy-start(f32[4,512,256]{1,2,0:T(8,128)} %copy-done) | copy-start | bytes 6291460
  293.3 4.3 copy-start.4
  297.6 2.4 copy-start.11
  297.7 2.4 copy-start.20
  307.9 36.4 %copy-start.6 = (f32[512,512]{0,1:T(8,128)S(1)}, f32[512,512]{0,1:T(8,128)}, u32[]{:S(2)}) copy-start(f32[512,512]{0,1:T(8,128)} %copy.36) | copy-start | bytes 3145732
  344.3 7.0 %copy-start.3 = (f32[4,512,256]{1,2,0:T(8,128)S(1)}, f32[4,512,256]{1,2,0:T(8,128)}, u32[]{:S(2)}) copy-start(f32[4,512,256]{1,2,0:T(8,128)} %copy-done) | copy-start | bytes 6291460
  344.3 7.0 %copy-start.13 = (f32[4,512,256]{1,2,0:T(8,128)S(1)}, f32[4,512,256]{1,2,0:T(8,128)}, u32[]{:S(2)}) copy-start(f32[4,512,256]{1,2,0:T(8,128)} %fusion.1) | copy-start | bytes 6291460
  344.3 7.0 %copy-start.16 = (bf16[512,4,128]{2,0,1:T(8,128)(2,1)S(1)}, bf16[512,4,128]{2,0,1:T(8,128)(2,1)}, u32[]{:S(2)}) copy-start(bf16[512,4,128]{2,0,1:T(8,128)(2,1)} %copy-done.14) | copy-start | bytes 1572868
  351.3 1.5 copy-start.12
  351.4 2.8 copy-start.22
  351.4 2.8 copy-start.28
  354.2 11.5 %copy-start.23 = (bf16[512,4,128]{0,2,1:T(8,128)(2,1)}, bf16[512,4,128]{0,2,1:T(8,128)(2,1)S(1)}, u32[]{:S(2)}) copy-start(bf16[512,4,128]{0,2,1:T(8,128)(2,1)S(1)} %fusion.28) | copy-start | bytes 1572868
  382.4 5.1 copy-start.24
  382.4 150.1 %reduce-scatter.5.cloned.1.call-start = ((), (), s32[]{:S(2)}) async-start(), calls=%async_computation.5 | async-start | bytes 5242880 | tf_op jit(solution)/shard_map/reduce_scatter | solution.py:210
  382.7 4.8 copy-start.21
  387.5 5.9 %copy-start.8 = (bf16[32,128,512]{2,1,0:T(8,128)(2,1)S(1)}, bf16[32,128,512]{2,1,0:T(8,128)(2,1)}, u32[]{:S(2)}) copy-start(bf16[32,128,512]{2,1,0:T(8,128)(2,1)} %copy-done.7) | copy-start | bytes 12582916
  (3 other events, 3.6 us)
Sparse Core Ops, SparseCore 0:
  10.2 72.0 all-gather.12
  84.6 45.1 all-gather.10
  132.6 52.1 all-gather.14
  192.9 110.4 all-gather.16
  382.5 99.3 reduce-scatter.6
  484.8 47.7 reduce-scatter.4
